TPU v7x, 32 devices: a whole 2x2x4 slice. The times are simulated.
32 devices in a mesh: path: 8 (over z, x), shard: 4 (over y, core).
Axes of the slice: x: 2, y: 2, z: 4, core: 2. Of those that a mesh axis runs over, the one named last changes fastest.
Arguments:
- master: float32 [2, 4096, 2048], P(None, ('path', 'shard')), may hold values from -6 to 6
- momentum: float32 [2, 4096, 2048], P(None, ('path', 'shard')), may hold values from -2 to 2
- routes: int32 [8, 1], replicated, may hold values from 0 to 1
- counts: int32 [8], replicated, may hold values from 1 to 8
- tokens: bfloat16 [12288, 4096], P(('path', 'shard')), may hold values from -6 to 6
- cotangent: bfloat16 [12288, 2048], P(('path', 'shard')), may hold values from -6 to 6
Outputs:
- master_new: float32 [2, 4096, 2048], P(None, ('path', 'shard'))
- momentum_new: float32 [2, 4096, 2048], P(None, ('path', 'shard'))
Inputs may be any that keep to these rules, and one draw needn't show every extreme that they name: `routes`: every module is read by at least one path.
All inputs are finite; a program needn't handle non-finite values.
Results may differ from a plain program's by a relative error of at most 0.0032.
Values may be sent and summed in bfloat16 or wider, within the bound.
No kernel may reach another device: no remote copies, remote signals or barrier semaphores. Data moves between devices by JAX's collectives and lax.ppermute only.
A program may use at most 128 MiB of HBM per device.

v0:
```python
import jax
import jax.numpy as jnp
from jax import lax
from jax.sharding import PartitionSpec as P


def local(master, momentum, routes, counts, tokens, cotangent):
    path_count = routes.shape[0]
    shards = lax.axis_size("shard")
    modules = master.shape[0]
    rows_block = master.shape[1]
    feat_width = master.shape[2]
    tok_rows = tokens.shape[0]
    model_width = tokens.shape[1]
    inv_root = model_width ** (-0.5)
    chosen = routes[:, 0]
    onehot = (chosen[None, :] == jnp.arange(modules, dtype=jnp.int32)[:, None]).astype(jnp.float32)
    outgoing = jnp.take(master.astype(jnp.bfloat16), chosen, axis=0)
    local_rows = lax.all_to_all(outgoing, "path", split_axis=0, concat_axis=0, tiled=True)
    local_weight = local_rows.reshape(path_count * rows_block, feat_width)
    permuted = tokens.reshape(tok_rows, path_count, shards, rows_block)
    permuted = permuted.transpose(0, 2, 1, 3).reshape(tok_rows, model_width)
    columns = lax.all_to_all(permuted, "shard", split_axis=1, concat_axis=0, tiled=True)
    columns_part = permuted
    pre_sum = jnp.dot(
        columns_part,
        lax.all_gather(local_weight, "shard", axis=0, tiled=True),
        preferred_element_type=jnp.float32,
    )
    pre_act = pre_sum * inv_root
    gate_value = jax.nn.sigmoid(pre_act)
    signal = (
        cotangent.astype(jnp.float32) * gate_value * (1.0 + pre_act * (1.0 - gate_value))
    ).astype(jnp.bfloat16)
    columns_part = columns
    product = lax.dot_general(
        columns_part,
        lax.all_gather(signal, "shard", axis=0, tiled=True),
        (((0,), (0,)), ((), ())),
        preferred_element_type=jnp.float32,
    )
    path_grad = (
        (product * inv_root).astype(jnp.bfloat16).reshape(path_count, rows_block, feat_width)
    )
    received = lax.all_to_all(path_grad, "path", split_axis=0, concat_axis=0, tiled=True)
    mixing = onehot * counts.astype(jnp.float32)[None, :]
    mixing = mixing / jnp.sum(mixing, axis=1, keepdims=True)
    flat_recv = received.reshape(path_count, rows_block * feat_width).astype(jnp.float32)
    outer_grad = jnp.dot(mixing, flat_recv, precision=lax.Precision.HIGHEST).reshape(
        modules, rows_block, feat_width
    )
    momentum_new = 0.9 * momentum + outer_grad
    master_new = master - 0.7 * (outer_grad + 0.9 * momentum_new)
    return (master_new, momentum_new)


def solution(mesh):
    placed = (
        P(None, ("path", "shard"), None),
        P(None, ("path", "shard"), None),
        P(),
        P(),
        P(("path", "shard"), None),
        P(("path", "shard"), None),
    )
    return jax.shard_map(
        local,
        mesh=mesh,
        in_specs=placed,
        out_specs=(P(None, ("path", "shard"), None), P(None, ("path", "shard"), None)),
        check_vma=False,
    )
```

profile of v0, /device:TPU:0, one launch (start us, length us, event | category | flops | bytes accessed | tf_op | source)
XLA Modules:
  0.0 444.9 jit_solution(9973681836863088704)
XLA Ops:
  7.2 0.0 all-gather.3.cloned.1.call-start
  7.2 0.7 fusion.16
  7.9 0.7 and_bitcast_fusion
  8.5 1.7 convert_element_type.22
  10.3 2.8 gather_fusion
  13.0 2.7 broadcast_select_fusion
  15.7 100.3 %all_to_all.29 = bf16[8,128,2048]{2,1,0:T(8,128)(2,1)} all-to-all(bf16[8,128,2048]{2,1,0:T(8,128)(2,1)S(1)} %broadcast_select_fusion), channel_id=1, replica_groups=mesh['path'=8,'shard'=4] {'path'}, dimensions={0} | all-to-all | bytes 8388608 | tf_op jit(solution)/shard_map/all_to_all | solution.py:19
  116.0 0.0 copy-start
  116.0 0.0 all-gather.3.cloned.1.call-update
  116.1 0.0 all-gather.5.cloned.1.call-start
  116.1 1.8 copy-done
  117.9 2.8 copy.27
  120.7 2.7 copy.28
  123.5 2.8 copy.26
  126.3 94.9 %all-gather.3.cloned.1.call-done = bf16[4096,2048]{1,0:T(8,128)(2,1)} async-done(((bf16[1024,2048]{1,0:T(8,128)(2,1)}), bf16[4096,2048]{1,0:T(8,128)(2,1)}) %all-gather.3.cloned.1.call-update) | async-done | bytes 16777232 | tf_op jit(solution)/shard_map/all_gather | solution.py:27
  221.2 14.3 %fusion.5 = bf16[384,2048]{0,1:T(8,128)(2,1)} fusion(bf16[384,2048]{0,1:T(8,128)(2,1)} %copy.26, bf16[4096,2048]{1,0:T(8,128)(2,1)} %all-gather.3.cloned.1.call-done, bf16[384,4096]{0,1:T(8,128)(2,1)S(1)} %bitcast.51), kind=kOutput, calls=%fused_computation.11 | convolution fusion | flops 6451101696 | bytes 23068672 | tf_op jit(solution)/shard_map/dot_general | solution.py:25
  235.5 0.0 all-gather.5.cloned.1.call-update
  235.5 69.7 %all_to_all.30 = bf16[384,4,1024]{0,2,1:T(8,128)(2,1)} all-to-all(bf16[384,4,1024]{0,2,1:T(8,128)(2,1)S(1)} %bitcast.52), channel_id=1, replica_groups=mesh['path'=8,'shard'=4] {'shard'}, dimensions={1} | all-to-all | bytes 6291456 | tf_op jit(solution)/shard_map/all_to_all | solution.py:23
  305.1 3.2 copy.30
  308.4 2.6 all-gather.5.cloned.1.call-done
  311.0 11.1 %multiply_convert_fusion = bf16[2048,1024]{0,1:T(8,128)(2,1)} fusion(bf16[1536,2048]{0,1:T(8,128)(2,1)} %all-gather.5.cloned.1.call-done, bf16[1536,1024]{1,0:T(8,128)(2,1)S(1)} %bitcast.56), kind=kOutput, calls=%fused_computation.1 | convolution fusion | flops 6446645248 | bytes 13631488 | tf_op jit(solution)/shard_map/dot_general | solution.py:36
  322.1 0.0 copy-start.2
  322.1 0.0 copy-start.3
  322.1 0.0 copy-start.1
  322.1 5.6 %all-to-all-start.2 = ((bf16[8,128,2048]{2,1,0:T(8,128)(2,1)}), bf16[8,128,2048]{2,1,0:T(8,128)(2,1)}, u32[]{:S(2)}, u32[]{:S(2)}) async-start(bf16[8,128,2048]{2,1,0:T(8,128)(2,1)} %bitcast.55), calls=%async_computation.2 | async-start | bytes 8388608 | tf_op jit(solution)/shard_map/all_to_all | solution.py:45
  327.8 0.0 copy-done.2
  327.8 0.0 copy-done.3
  327.8 0.1 fusion.10
  327.9 93.6 %all-to-all-done.2 = bf16[8,128,2048]{2,1,0:T(8,128)(2,1)} async-done(((bf16[8,128,2048]{2,1,0:T(8,128)(2,1)}), bf16[8,128,2048]{2,1,0:T(8,128)(2,1)}, u32[]{:S(2)}, u32[]{:S(2)}) %all-to-all-start.2) | async-done | bytes 4194336 | tf_op jit(solution)/shard_map/all_to_all | solution.py:45
  421.5 0.0 copy-done.1
  421.5 11.5 %fusion.6 = (f32[2,128,2048]{2,0,1:T(2,128)S(1)}, f32[2,128,2048]{2,0,1:T(2,128)S(1)}) fusion(f32[2,128,2048]{2,1,0:T(8,128)} %param.7, f32[2,128,2048]{2,1,0:T(8,128)S(1)} %copy-done.1, f32[2]{0:T(128)S(1)} %fusion.10, f32[8]{0:T(128)S(1)} %convert_element_type.20, s32[8]{0:T(128)S(1)} %bitcast.58, bf16[1,8,128,2048]{3,2,1,0:T(8,128)(2,1)} %bitcast.19), kind=kOutput, calls=%fused_computation.14 | convolution fusion | flops 53477424 | bytes 12582984 | tf_op jit(solution)/shard_map/dot_general | solution.py:49
  433.0 2.5 copy.33
  435.5 2.5 copy.34
  (2 shorter events, 0.0 us)
Async XLA Ops:
  7.2 214.0 %all-gather.3.cloned.1.call-start = ((), (), s32[]{:S(2)}) async-start(), calls=%async_computation.3 | async-start | bytes 20971520 | tf_op jit(solution)/shard_map/all_gather | solution.py:27
  116.0 1.9 copy-start
  116.1 194.9 %all-gather.5.cloned.1.call-start = ((), (), s32[]{:S(2)}) async-start(), calls=%async_computation.4 | async-start | bytes 7864320 | tf_op jit(solution)/shard_map/all_gather | solution.py:38
  322.1 5.7 %copy-start.2 = (s32[8]{0:T(128)S(1)}, s32[8]{0:T(128)}, u32[]{:S(2)}) copy-start(s32[8]{0:T(128)} %param.9) | copy-start | bytes 100
  322.1 5.7 %copy-start.3 = (s32[8,1]{0,1:T(1,128)S(1)}, s32[8,1]{0,1:T(1,128)}, u32[]{:S(2)}) copy-start(s32[8,1]{0,1:T(1,128)} %param.8) | copy-start | bytes 100
  322.1 99.3 %copy-start.1 = (f32[2,128,2048]{2,1,0:T(8,128)S(1)}, f32[2,128,2048]{2,1,0:T(8,128)}, u32[]{:S(2)}) copy-start(f32[2,128,2048]{2,1,0:T(8,128)} %param.6) | copy-start | bytes 6291460
  322.1 99.3 %all-to-all-start.2 = ((bf16[8,128,2048]{2,1,0:T(8,128)(2,1)}), bf16[8,128,2048]{2,1,0:T(8,128)(2,1)}, u32[]{:S(2)}, u32[]{:S(2)}) async-start(bf16[8,128,2048]{2,1,0:T(8,128)(2,1)} %bitcast.55), calls=%async_computation.2 | async-start | bytes 8388608 | tf_op jit(solution)/shard_map/all_to_all | solution.py:45
Sparse Core Ops, SparseCore 0:
  116.2 104.9 all-gather.2
  235.6 75.3 all-gather.4
where the time goes:
time: 445 us
  waiting for transfers between devices  191 us (43%)
  blocking collectives  170 us (38%)
  matrix products  36.9 us (8%)
  local copies, waits for them, and re-layouts  21.2 us (5%)
  between operations  14.1 us (3%)
  other arithmetic  5.83 us (1%)
  starting transfers between devices  5.72 us (1%)
    all_to_all x1, blocking collectives, local(): lax.all_to_all(outgoing, 'path', split_axis=0, concat_axis=0, tiled=True)  100 us
    all_gather x1, waiting for transfers between devices, local(): lax.all_gather(local_weight, 'shard', axis=0, tiled=True)  94.9 us
    all_to_all x1, waiting for transfers between devices, local(): lax.all_to_all(path_grad, 'path', split_axis=0, concat_axis=0, tiled=True)  93.6 us
    all_to_all x1, blocking collectives, local(): lax.all_to_all(permuted, 'shard', split_axis=1, concat_axis=0, tiled=True)  69.7 us
    dot_general x1, matrix products, local(): jnp.dot(columns_part, lax.all_gather(local_weight, 'shard', axis=0, tiled...  14.3 us
    unnamed x12, local copies, waits for them, and re-layouts  12.5 us
    dot_general x1, matrix products, local(): jnp.dot(mixing, flat_recv, precision=lax.Precision.HIGHEST)  11.5 us
    dot_general x1, matrix products, local(): lax.dot_general(columns_part, lax.all_gather(signal, 'shard', axis=0, til...  11.1 us
  transfers between devices with their start and end apart: 3, of which 3 were waited for; matrix products, arithmetic and copies ran while one was open for 3% of the time, Pallas kernels for 0%

commit v1 on v0

--- a/solution.py
+++ b/solution.py
@@ -2,6 +2,19 @@
 import jax.numpy as jnp
 from jax import lax
 from jax.sharding import PartitionSpec as P
+
+
+def ring_gather(x, axis, dim):
+    ways = lax.axis_size(axis)
+    up = [(d, (d + 1) % ways) for d in range(ways)]
+    down = [(d, (d - 1) % ways) for d in range(ways)]
+    earlier, later = ([x], [x])
+    for _ in range(ways // 2):
+        earlier.append(lax.ppermute(earlier[-1], axis, up))
+    for _ in range((ways - 1) // 2):
+        later.append(lax.ppermute(later[-1], axis, down))
+    line = jnp.concatenate([*earlier[::-1], *later[1:]], axis=dim)
+    return jnp.roll(line, (lax.axis_index(axis) - ways // 2) * x.shape[dim], axis=dim)
 
 
 def local(master, momentum, routes, counts, tokens, cotangent):
@@ -23,9 +36,7 @@
     columns = lax.all_to_all(permuted, "shard", split_axis=1, concat_axis=0, tiled=True)
     columns_part = permuted
     pre_sum = jnp.dot(
-        columns_part,
-        lax.all_gather(local_weight, "shard", axis=0, tiled=True),
-        preferred_element_type=jnp.float32,
+        columns_part, ring_gather(local_weight, "shard", 0), preferred_element_type=jnp.float32
     )
     pre_act = pre_sum * inv_root
     gate_value = jax.nn.sigmoid(pre_act)

time: 445 us -> 518 us (1.16)
  local copies, waits for them, and re-layouts: 21.2 us -> 56.6 us
  waiting for transfers between devices: 191 us -> 226 us
    ppermute x0 -> x3, waiting for transfers between devices: none -> 130 us  [the longest x2 130 us: ring_gather(): earlier.append(lax.ppermute(earlier[-1], axis, up))]
    all_gather x1 -> x0, waiting for transfers between devices: 94.9 us -> none  [local(): lax.all_gather(local_weight, 'shard', axis=0, tiled=True)]
    unnamed x12 -> x21, local copies, waits for them, and re-layouts: 12.5 us -> 43.6 us
  transfers between devices with their start and end apart: 3 -> 5, of which waited for: 3 -> 4; matrix products, arithmetic and copies ran while one was open for 3% -> 5% of each run, Pallas kernels for 0% -> 0%
where the time goes in v1:
time: 518 us; the launch traced here: 517 us
  waiting for transfers between devices  226 us (44%)
  blocking collectives  172 us (33%)
  local copies, waits for them, and re-layouts  56.6 us (11%)
  matrix products  36.8 us (7%)
  between operations  14.1 us (3%)
  starting transfers between devices  6.46 us (1%)
  other arithmetic  5.83 us (1%)
    ppermute x2, waiting for transfers between devices, ring_gather(): earlier.append(lax.ppermute(earlier[-1], axis, up))  130 us
    all_to_all x1, blocking collectives, local(): lax.all_to_all(outgoing, 'path', split_axis=0, concat_axis=0, tiled=True)  101 us
    all_to_all x1, waiting for transfers between devices, local(): lax.all_to_all(path_grad, 'path', split_axis=0, concat_axis=0, tiled=True)  93.7 us
    all_to_all x1, blocking collectives, local(): lax.all_to_all(permuted, 'shard', split_axis=1, concat_axis=0, tiled=True)  70.9 us
    unnamed x21, local copies, waits for them, and re-layouts  43.6 us
    dot_general x1, matrix products, local(): jnp.dot(columns_part, ring_gather(local_weight, 'shard', 0), preferred_el...  14.1 us
    dot_general x1, matrix products, local(): jnp.dot(mixing, flat_recv, precision=lax.Precision.HIGHEST)  11.5 us
    dot_general x1, matrix products, local(): lax.dot_general(columns_part, lax.all_gather(signal, 'shard', axis=0, til...  11.2 us
  transfers between devices with their start and end apart: 5, of which 4 were waited for; matrix products, arithmetic and copies ran while one was open for 5% of the time, Pallas kernels for 0%

profile of v1, /device:TPU:0, one launch (start us, length us, event | category | flops | bytes accessed | tf_op | source)
XLA Modules:
  0.0 517.0 jit_solution(8054999074292243938)
XLA Ops:
  7.2 0.0 all-gather.2.cloned.1.call-start
  7.2 0.7 fusion.24
  7.9 0.7 and_bitcast_fusion
  8.5 1.7 convert_element_type.22
  10.3 2.8 gather_fusion
  13.1 2.7 broadcast_select_fusion
  15.7 0.0 copy-start
  15.7 100.6 %all_to_all.29 = bf16[8,128,2048]{2,1,0:T(8,128)(2,1)} all-to-all(bf16[8,128,2048]{2,1,0:T(8,128)(2,1)S(1)} %broadcast_select_fusion), channel_id=1, replica_groups=mesh['path'=8,'shard'=4] {'path'}, dimensions={0} | all-to-all | bytes 8388608 | tf_op jit(solution)/shard_map/all_to_all | solution.py:32
  116.3 0.0 collective-permute-start
  116.3 48.2 %collective-permute-done = bf16[1024,2048]{1,0:T(8,128)(2,1)} collective-permute-done((bf16[1024,2048]{1,0:T(8,128)(2,1)}, bf16[1024,2048]{1,0:T(8,128)(2,1)}, u32[]{:S(2)}, u32[]{:S(2)}) %collective-permute-start) | collective-permute-done | bytes 4194336 | tf_op jit(solution)/shard_map/ppermute | solution.py:13
  164.6 0.0 collective-permute-start.1
  164.6 1.7 collective-permute-start.2
  166.3 0.0 copy-done
  166.3 2.8 copy.27
  169.1 2.2 copy.28
  171.4 2.6 copy.26
  173.9 81.9 %collective-permute-done.1 = bf16[1024,2048]{1,0:T(8,128)(2,1)} collective-permute-done((bf16[1024,2048]{1,0:T(8,128)(2,1)}, bf16[1024,2048]{1,0:T(8,128)(2,1)}, u32[]{:S(2)}, u32[]{:S(2)}) %collective-permute-start.1) | collective-permute-done | bytes 4194336 | tf_op jit(solution)/shard_map/ppermute | solution.py:13
  255.9 4.7 constant_dynamic-update-slice_fusion.7
  260.6 4.7 constant_dynamic-update-slice_fusion.6
  265.3 4.7 constant_dynamic-update-slice_fusion.5
  270.1 0.0 collective-permute-done.2
  270.1 4.7 constant_dynamic-update-slice_fusion.4
  274.8 4.7 constant_dynamic-update-slice_fusion.3
  279.5 4.7 constant_dynamic-update-slice_fusion.2
  284.2 4.7 constant_dynamic-update-slice_fusion.1
  289.0 0.0 copy-start.2
  289.0 4.8 constant_dynamic-update-slice_fusion
  293.8 0.0 copy-done.2
  293.8 14.1 %fusion.10 = bf16[384,2048]{0,1:T(8,128)(2,1)} fusion(bf16[384,2048]{0,1:T(8,128)(2,1)S(1)} %copy-done.2, bf16[384,4096]{0,1:T(8,128)(2,1)S(1)} %bitcast.49, bf16[8192,2048]{1,0:T(8,128)(2,1)} %constant_dynamic-update-slice_fusion, s32[]{:T(128)S(6)} %select_n.27), kind=kOutput, calls=%fused_computation.13 | convolution fusion | flops 6451101696 | bytes 23068676 | tf_op jit(solution)/shard_map/dot_general | solution.py:38
  307.9 0.0 all-gather.2.cloned.1.call-update
  308.0 70.9 %all_to_all.30 = bf16[384,4,1024]{0,2,1:T(8,128)(2,1)} all-to-all(bf16[384,4,1024]{0,2,1:T(8,128)(2,1)S(1)} %bitcast.50), channel_id=1, replica_groups=mesh['path'=8,'shard'=4] {'shard'}, dimensions={1} | all-to-all | bytes 6291456 | tf_op jit(solution)/shard_map/all_to_all | solution.py:36
  378.9 3.2 copy.30
  382.1 1.9 all-gather.2.cloned.1.call-done
  383.9 11.2 %multiply_convert_fusion = bf16[2048,1024]{0,1:T(8,128)(2,1)} fusion(bf16[1536,2048]{0,1:T(8,128)(2,1)} %all-gather.2.cloned.1.call-done, bf16[1536,1024]{1,0:T(8,128)(2,1)S(1)} %bitcast.54), kind=kOutput, calls=%fused_computation.3 | convolution fusion | flops 6446645248 | bytes 13631488 | tf_op jit(solution)/shard_map/dot_general | solution.py:47
  395.1 0.0 copy-start.3
  395.1 0.0 copy-start.4
  395.1 0.0 copy-start.1
  395.1 4.7 all-to-all-start.2
  399.8 0.0 copy-done.3
  399.8 0.0 copy-done.4
  399.8 0.1 fusion.17
  399.9 93.7 %all-to-all-done.2 = bf16[8,128,2048]{2,1,0:T(8,128)(2,1)} async-done(((bf16[8,128,2048]{2,1,0:T(8,128)(2,1)}), bf16[8,128,2048]{2,1,0:T(8,128)(2,1)}, u32[]{:S(2)}, u32[]{:S(2)}) %all-to-all-start.2) | async-done | bytes 4194336 | tf_op jit(solution)/shard_map/all_to_all | solution.py:56
  493.6 0.0 copy-done.1
  493.6 11.5 %fusion.13 = (f32[2,128,2048]{2,0,1:T(2,128)S(1)}, f32[2,128,2048]{2,0,1:T(2,128)S(1)}) fusion(f32[2,128,2048]{2,1,0:T(8,128)} %param.7, f32[2,128,2048]{2,1,0:T(8,128)S(1)} %copy-done.1, f32[2]{0:T(128)S(1)} %fusion.17, f32[8]{0:T(128)S(1)} %convert_element_type.20, s32[8]{0:T(128)S(1)} %bitcast.56, bf16[1,8,128,2048]{3,2,1,0:T(8,128)(2,1)} %bitcast.19), kind=kOutput, calls=%fused_computation.16 | convolution fusion | flops 53477424 | bytes 12582984 | tf_op jit(solution)/shard_map/dot_general | solution.py:60
  505.1 2.5 copy.33
  507.7 2.5 copy.34
  (2 shorter events, 0.0 us)
Async XLA Ops:
  7.2 376.8 %all-gather.2.cloned.1.call-start = ((), (), s32[]{:S(2)}) async-start(), calls=%async_computation.3 | async-start | bytes 7864320 | tf_op jit(solution)/shard_map/all_gather | solution.py:49
  15.7 150.6 %copy-start = (bf16[384,4096]{1,0:T(8,128)(2,1)S(1)}, bf16[384,4096]{1,0:T(8,128)(2,1)}, u32[]{:S(2)}) copy-start(bf16[384,4096]{1,0:T(8,128)(2,1)} %param.10) | copy-start | bytes 9437188
  116.3 48.2 %collective-permute-start = (bf16[1024,2048]{1,0:T(8,128)(2,1)}, bf16[1024,2048]{1,0:T(8,128)(2,1)}, u32[]{:S(2)}, u32[]{:S(2)}) collective-permute-start(bf16[1024,2048]{1,0:T(8,128)(2,1)} %bitcast.4), channel_id=1, source_target_pairs={{0,1},{1,2},{2,3},{3,0},{4,5},{5,6},{6,7},{7,4},{8,9},{9,10},{10,1... | collective-permute-start | bytes 12582920 | tf_op jit(solution)/shard_map/ppermute | solution.py:13
  164.6 91.3 %collective-permute-start.1 = (bf16[1024,2048]{1,0:T(8,128)(2,1)}, bf16[1024,2048]{1,0:T(8,128)(2,1)}, u32[]{:S(2)}, u32[]{:S(2)}) collective-permute-start(bf16[1024,2048]{1,0:T(8,128)(2,1)} %collective-permute-done), channel_id=1, source_target_pairs={{0,1},{1,2},{2,3},{3,0},{4,5},{5,6},{6,7},{7,4},{8,9},{9,10},{10,1... | collective-permute-start | bytes 12582920 | tf_op jit(solution)/shard_map/ppermute | solution.py:13
  164.6 105.5 %collective-permute-start.2 = (bf16[1024,2048]{1,0:T(8,128)(2,1)}, bf16[1024,2048]{1,0:T(8,128)(2,1)}, u32[]{:S(2)}, u32[]{:S(2)}) collective-permute-start(bf16[1024,2048]{1,0:T(8,128)(2,1)} %bitcast.4), channel_id=1, source_target_pairs={{0,3},{1,0},{2,1},{3,2},{4,7},{5,4},{6,5},{7,6},{8,11},{9,8},{10,9... | collective-permute-start | bytes 12582920 | tf_op jit(solution)/shard_map/ppermute | solution.py:15
  289.0 4.8 copy-start.2
  395.1 4.7 copy-start.3
  395.1 4.7 copy-start.4
  395.1 98.6 %copy-start.1 = (f32[2,128,2048]{2,1,0:T(8,128)S(1)}, f32[2,128,2048]{2,1,0:T(8,128)}, u32[]{:S(2)}) copy-start(f32[2,128,2048]{2,1,0:T(8,128)} %param.6) | copy-start | bytes 6291460
  395.1 98.5 %all-to-all-start.2 = ((bf16[8,128,2048]{2,1,0:T(8,128)(2,1)}), bf16[8,128,2048]{2,1,0:T(8,128)(2,1)}, u32[]{:S(2)}, u32[]{:S(2)}) async-start(bf16[8,128,2048]{2,1,0:T(8,128)(2,1)} %bitcast.53), calls=%async_computation.2 | async-start | bytes 8388608 | tf_op jit(solution)/shard_map/all_to_all | solution.py:56
Sparse Core Ops, SparseCore 0:
  308.1 75.7 all-gather.1
